TPU v7x, 32 devices: a whole 2x2x4 slice. The times are simulated.
32 devices in a mesh: seq: 16 (over z, y, x), head: 2 (over core).
Axes of the slice: x: 2, y: 2, z: 4, core: 2. Of those that a mesh axis runs over, the one named last changes fastest.
Arguments:
- query_tok: bfloat16 [6144, 1536], P('seq', 'head'), may hold values from -110 to 110
- key_tok: bfloat16 [6144, 1536], P('seq', 'head'), may hold values from -5 to 5
- value_tok: bfloat16 [6144, 1536], P('seq', 'head'), may hold values from -6 to 6
- out_weight: bfloat16 [3072, 1536], P(None, 'head'), may hold values from -0.15625 to 0.15625
- grad_out: bfloat16 [6144, 3072], P('seq', 'head'), may hold values from -6 to 6
- tile_pairs: int32 [16, 7], P('seq'), may hold values from -1 to 15, as said below
Outputs:
- mixed_out: bfloat16 [6144, 3072], P('seq', 'head')
- grad_query: bfloat16 [6144, 1536], P('seq', 'head')
- grad_key: bfloat16 [6144, 1536], P('seq', 'head')
- grad_value: bfloat16 [6144, 1536], P('seq', 'head')
Inputs may be any that keep to these rules, and one draw needn't show every extreme that they name: `tile_pairs`: slot j of tile g holds g + o_j or -1, with offsets o = (0, 1, -1, 8, -8, 16, -16); slot 0 always holds g; the list is symmetric: b is in the list of g exactly when g is in the list of b.
All inputs are finite; a program needn't handle non-finite values.
Results may differ from a plain program's by a relative error of at most 0.025.
Values may be sent and summed in bfloat16 or wider, within the bound.
A program may use at most 192 MiB of HBM per device.

v0:
```python
import functools

import jax
import jax.numpy as jnp
from jax import lax
from jax.experimental import pallas as pl
from jax.experimental.pallas import tpu as pltpu
from jax.sharding import PartitionSpec as P

HD = 128
GW_T = 8
MASKED = -1e30
LOG2E = 1.4426950408889634
MESH = pl.DeviceIdType.MESH
F32 = jnp.float32
BF16 = jnp.bfloat16


def slot_groups(tile_count):
    frame_tiles = min(4, tile_count // 8) * GW_T
    offsets = (0, 1, -1, GW_T, -GW_T, frame_tiles, -frame_tiles)
    groups = []
    for column, offset in enumerate(offsets):
        if abs(offset) >= tile_count:
            continue
        for group in groups:
            if (group[0] - offset) % tile_count == 0:
                group[1] = True
                group[2].append(column)
                break
        else:
            groups.append([offset, False, [column]])
    return groups


def dot(a, b, da, db):
    return lax.dot_general(a, b, (((da,), (db,)), ((), ())), preferred_element_type=F32)


def kernel(
    groups, tile_count, scale,
    pairs, q_in, k_in, v_in, w_in, g_in,
    mixed, gq, gk, gv,
    kv, qb, wb, gown, goth, gacc, dob, att, probs, acc, tsend, trecv, msend, mrecv,
    load_sem, kv_send, kv_recv, t_send, t_recv, x_send, x_recv,
):
    g = lax.axis_index("seq")
    c = lax.axis_index("head")
    other = 1 - c
    heads = qb.shape[0]
    rows = qb.shape[1]
    half = gown.shape[1]
    slots = len(groups)

    def place(step, wraps):
        at = g + step
        if wraps:
            return lax.rem(at + tile_count, tile_count), None
        ok = jnp.logical_and(at >= 0, at < tile_count)
        return jnp.clip(at, 0, tile_count - 1), ok

    def when(ok, fn):
        if ok is None:
            fn()
        else:
            pl.when(ok)(fn)

    source = [place(o, w) for o, w, _ in groups]
    target = [place(-o, w) for o, w, _ in groups]
    swaps = [s for s, (_, w, _) in enumerate(groups) if w]
    swap = swaps[0] if swaps else None
    hands_on = [None] * slots
    middle = tile_count // 2
    if swap is not None:
        for s, (o, _, _) in enumerate(groups):
            if abs(o) != 1:
                continue
            ends, near = ((tile_count - 1, middle), (0, middle - 1))[o > 0]
            relay = g == ends
            hands_on[s] = relay
            to, ok = target[s]
            crossing = g == (2 * middle - 1) - near
            target[s] = (
                jnp.where(relay, near, to),
                jnp.logical_or(relay, jnp.logical_and(ok, jnp.logical_not(crossing))),
            )
            at, ok = source[s]
            source[s] = (jnp.where(g == near, ends, at), ok)
    direct = [
        ok if hand is None else jnp.logical_and(ok, jnp.logical_not(hand))
        for (_, ok), hand in zip(target, hands_on)
    ]
    relays = [s for s in range(slots) if hands_on[s] is not None]
    relaying = None
    for s in relays:
        relaying = hands_on[s] if relaying is None else jnp.logical_or(relaying, hands_on[s])
    order = [0] + ([swap] if swap is not None else [])
    order += [s for s in range(slots) if s not in order]
    ahead = min(2, heads)

    barrier = pltpu.get_barrier_semaphore()
    pl.semaphore_signal(barrier, inc=1, device_id=(g, other), device_id_type=MESH)
    peers = 1
    for to, ok in target[1:] + source[1:]:

        def greet(to=to):
            pl.semaphore_signal(barrier, inc=1, device_id=(to, c), device_id_type=MESH)

        when(ok, greet)
        peers = peers + (1 if ok is None else ok.astype(jnp.int32))

    loads = []

    def load(src, dst):
        copy = pltpu.make_async_copy(src, dst, load_sem.at[len(loads)])
        copy.start()
        loads.append(copy)
        return copy

    kv_loads = []
    for h in range(heads):
        cols = pl.ds(h * HD, HD)
        kv_loads.append(
            (load(k_in.at[:, cols], kv.at[h, 0, 0]), load(v_in.at[:, cols], kv.at[h, 0, 1]))
        )
    own_load = load(g_in, gown)
    w_load = load(w_in, wb)
    q_loads = [load(q_in.at[:, pl.ds(h * HD, HD)], qb.at[h]) for h in range(heads)]

    pl.semaphore_wait(barrier, peers)

    def partner_copy(src, dst, i):
        return pltpu.make_async_remote_copy(
            src_ref=src, dst_ref=dst, send_sem=x_send.at[i], recv_sem=x_recv.at[i],
            device_id=(g, other), device_id_type=MESH,
        )

    def kv_copy(s, h, held=0):
        return pltpu.make_async_remote_copy(
            src_ref=kv.at[h, held], dst_ref=kv.at[h, s],
            send_sem=kv_send.at[s - 1, h], recv_sem=kv_recv.at[s - 1, h],
            device_id=(target[s][0], c), device_id_type=MESH,
        )

    def term_copy(s, h):
        return pltpu.make_async_remote_copy(
            src_ref=tsend.at[s - 1, h], dst_ref=trecv.at[s - 1, h],
            send_sem=t_send.at[s - 1, h], recv_sem=t_recv.at[s - 1, h],
            device_id=(source[s][0], c), device_id_type=MESH,
        )

    for h in range(heads):
        for copy in kv_loads[h]:
            copy.wait()
        for s in reversed(range(1, slots)):
            ok = direct[s]
            if h >= ahead and s != swap and relays:
                ok = jnp.logical_and(ok, jnp.logical_not(relaying))
            when(ok, lambda s=s, h=h: kv_copy(s, h).start())
    own_load.wait()
    grad_copy = partner_copy(gown, goth, 0)
    grad_copy.start()

    for s in range(1, slots):
        if source[s][1] is not None:

            def clear(s=s):
                def body(h, carry):
                    kv[h, s] = jnp.zeros(kv.shape[2:], BF16)
                    return carry

                lax.fori_loop(0, heads, body, 0)

            pl.when(jnp.logical_not(source[s][1]))(clear)

    w_load.wait()
    mine = pl.multiple_of(c * half, half)
    theirs = pl.multiple_of(other * half, half)

    def grad_own(h, carry):
        cols = pl.ds(pl.multiple_of(h * HD, HD), HD)
        gacc[h] = dot(gown[...], wb[pl.ds(mine, half), cols], 1, 0)
        return carry

    lax.fori_loop(0, heads, grad_own, 0)
    grad_copy.wait()

    def grad_other(h, carry):
        cols = pl.ds(pl.multiple_of(h * HD, HD), HD)
        dob[h] = (gacc[h] + dot(goth[...], wb[pl.ds(theirs, half), cols], 1, 0)).astype(BF16)
        return carry

    lax.fori_loop(0, heads, grad_other, 0)
    for copy in q_loads:
        copy.wait()

    biases = []
    for _, _, columns in groups:
        there = pairs[0, columns[0]]
        for column in columns[1:]:
            there = jnp.maximum(there, pairs[0, column])
        biases.append(jnp.where(there >= 0, 0.0, MASKED).astype(F32))
    rate = scale * LOG2E
    lag = heads

    def hand_back(r, h):
        term_copy(r, h).wait_recv()
        both = tsend[swap - 1, h].astype(F32) + trecv[r - 1, h].astype(F32)
        tsend[swap - 1, h] = both.astype(BF16)
        term_copy(swap, h).start()

    def head(h, carry):
        cols = pl.ds(pl.multiple_of(h * HD, HD), HD)
        q = qb[h]
        do = dob[h]
        top = None
        for s in order:
            if s:
                when(source[s][1], lambda s=s: kv_copy(s, h).wait_recv())
            if s and s == swap:
                for r in relays:
                    when(hands_on[r], lambda r=r: kv_copy(r, h, swap).start())
                    now = jnp.logical_and(jnp.logical_and(relaying, direct[r]), h + ahead < heads)
                    when(now, lambda r=r: kv_copy(r, h + ahead).start())
            scores = dot(kv[h, s, 0], q, 1, 1)
            probs[s] = scores
            peak = jnp.max(scores, axis=0, keepdims=True) + biases[s]
            top = peak if top is None else jnp.maximum(top, peak)
        total = None
        for s in range(slots):
            e = jnp.exp2((probs[s] - top) * rate + biases[s])
            probs[s] = e
            part = jnp.sum(e, axis=0, keepdims=True)
            total = part if total is None else total + part
        inverse = 1.0 / total
        out_t = None
        for s in range(slots):
            p = probs[s] * inverse
            probs[s] = p
            low = p.astype(BF16)
            part = dot(kv[h, s, 1], low, 0, 0)
            out_t = part if out_t is None else out_t + part
            term = dot(low, do, 1, 0)
            if s:
                tsend[s - 1, h, 1] = term.astype(BF16)
            else:
                acc[h, 1] = term
        delta = jnp.sum(do.astype(F32).T * out_t, axis=0, keepdims=True)
        att[:, cols] = out_t.T.astype(BF16)
        gq_t = None
        for s in range(slots):
            gp = dot(kv[h, s, 1], do, 1, 1)
            gs = (probs[s] * (gp - delta)).astype(BF16)
            term = dot(gs, q, 1, 0) * scale
            if s:
                tsend[s - 1, h, 0] = term.astype(BF16)
            else:
                acc[h, 0] = term
            part = dot(kv[h, s, 0], gs, 0, 0)
            gq_t = part if gq_t is None else gq_t + part
        gq[:, cols] = (gq_t * scale).T.astype(BF16)
        for s in reversed(range(1, slots)):
            ok = source[s][1]
            if s == swap and relays:
                ok = jnp.logical_not(relaying)
            when(ok, lambda s=s: term_copy(s, h).start())
        for r in relays:
            now = jnp.logical_and(hands_on[r], h >= lag)
            when(now, lambda r=r: hand_back(r, h - lag))
        return carry

    lax.fori_loop(0, heads, head, 0)

    def hand_back_rest(r):
        def body(h, carry):
            hand_back(r, h)
            return carry

        lax.fori_loop(heads - lag, heads, body, 0)

    for r in relays:
        when(hands_on[r], lambda r=r: hand_back_rest(r))

    wide = 256 if half % 256 == 0 else HD

    def project_other(j, carry):
        at = pl.multiple_of(j * wide, wide)
        msend[:, pl.ds(at, wide)] = dot(
            att[...], wb[pl.ds(pl.multiple_of(theirs + at, wide), wide), :], 1, 1
        ).astype(BF16)
        return carry

    lax.fori_loop(0, half // wide, project_other, 0)
    mixed_copy = partner_copy(msend, mrecv, 1)
    mixed_copy.start()

    def project_own(j, carry):
        at = pl.multiple_of(j * wide, wide)
        part = dot(att[...], wb[pl.ds(pl.multiple_of(mine + at, wide), wide), :], 1, 1)

        @pl.when(j == 0)
        def _():
            mixed_copy.wait_recv()

        mixed[:, pl.ds(at, wide)] = (part + mrecv[:, pl.ds(at, wide)].astype(F32)).astype(BF16)
        return carry

    lax.fori_loop(0, half // wide, project_own, 0)

    def finish(h, carry):
        cols = pl.ds(pl.multiple_of(h * HD, HD), HD)
        for s in reversed(range(1, slots)):

            def add(s=s):
                term_copy(s, h).wait_recv()
                acc[h] = acc[h] + trecv[s - 1, h].astype(F32)

            when(direct[s], add)
        gk[:, cols] = acc[h, 0].astype(BF16)
        gv[:, cols] = acc[h, 1].astype(BF16)
        return carry

    lax.fori_loop(0, heads, finish, 0)

    mixed_copy.wait_send()

    def drain(h, carry):
        for s in range(1, slots):
            when(target[s][1], lambda s=s: kv_copy(s, h).wait_send())
            when(source[s][1], lambda s=s: term_copy(s, h).wait_send())
        return carry

    lax.fori_loop(0, heads, drain, 0)


def on_device(query_tok, key_tok, value_tok, out_weight, grad_out, tile_pairs):
    rows, width = query_tok.shape
    heads = width // HD
    half = grad_out.shape[1]
    tile_count = lax.axis_size("seq")
    groups = slot_groups(tile_count)
    slots = len(groups)
    anywhere = pl.BlockSpec(memory_space=pl.ANY)
    in_vmem = pl.BlockSpec(memory_space=pltpu.VMEM)
    dma = pltpu.SemaphoreType.DMA
    near = (slots - 1, heads)
    return pl.pallas_call(
        functools.partial(kernel, groups, tile_count, HD ** (-0.5)),
        out_shape=(
            pltpu.VMEM((rows, half), BF16),
            pltpu.VMEM((rows, width), BF16),
            pltpu.VMEM((rows, width), BF16),
            pltpu.VMEM((rows, width), BF16),
        ),
        in_specs=[pl.BlockSpec(memory_space=pltpu.SMEM)] + [anywhere] * 5,
        out_specs=(in_vmem,) * 4,
        scratch_shapes=[
            pltpu.VMEM((heads, slots, 2, rows, HD), BF16),
            pltpu.VMEM((heads, rows, HD), BF16),
            pltpu.VMEM(out_weight.shape, BF16),
            pltpu.VMEM((rows, half), BF16),
            pltpu.VMEM((rows, half), BF16),
            pltpu.VMEM((heads, rows, HD), F32),
            pltpu.VMEM((heads, rows, HD), BF16),
            pltpu.VMEM((rows, width), BF16),
            pltpu.VMEM((slots, rows, rows), F32),
            pltpu.VMEM((heads, 2, rows, HD), F32),
            pltpu.VMEM(near + (2, rows, HD), BF16),
            pltpu.VMEM(near + (2, rows, HD), BF16),
            pltpu.VMEM((rows, half), BF16),
            pltpu.VMEM((rows, half), BF16),
            dma((3 * heads + 2,)),
            dma(near),
            dma(near),
            dma(near),
            dma(near),
            dma((2,)),
            dma((2,)),
        ],
        compiler_params=pltpu.CompilerParams(
            collective_id=0, has_side_effects=True, vmem_limit_bytes=52 * 2**20
        ),
        name="tile_attention",
    )(tile_pairs, query_tok, key_tok, value_tok, out_weight, grad_out)


def solution(mesh):
    in_specs = (
        P("seq", "head"),
        P("seq", "head"),
        P("seq", "head"),
        P(None, "head"),
        P("seq", "head"),
        P("seq", None),
    )
    out_specs = (P("seq", "head"), P("seq", "head"), P("seq", "head"), P("seq", "head"))
    return jax.shard_map(
        on_device, mesh=mesh, in_specs=in_specs, out_specs=out_specs, check_vma=False
    )
```

profile of v0, /device:TPU:0, one launch (start us, length us, event | category | flops | bytes accessed | tf_op | source)
XLA Modules:
  0.0 122.3 jit_solution(16596791277718814424)
XLA Ops:
  0.6 118.2 %tile_attention.1 = (bf16[384,1536]{1,0:T(8,128)(2,1)S(1)}, bf16[384,768]{1,0:T(8,128)(2,1)S(1)}, bf16[384,768]{1,0:T(8,128)(2,1)S(1)}, bf16[384,768]{1,0:T(8,128)(2,1)S(1)}) custom-call(s32[1,7]{1,0:T(1,128)} %pairs.1, bf16[384,768]{1,0:T(8,128)(2,1)} %q_in.1, bf16[384,768]{1,0:T(8,128)(2,1)} %k_in.1, bf16[384,768]{1,0:T(8,128)(2,1)} %v_in.1, ...), custom_call_target="tpu_custom_call" | custom-call | tf_op jit(solution)/shard_map/tile_attention/pallas_call | solution.py:347
  118.8 1.0 copy.14
  119.8 0.8 copy.15
  120.7 0.8 copy.16
  121.5 0.8 copy.17
where the time goes:
time: 122 us
  Pallas kernels  118 us (97%)
  local copies, waits for them, and re-layouts  3.46 us (3%)
    pallas_call x1, Pallas kernels, on_device(): pl.pallas_call(functools.partial(kernel, groups, tile_count, HD ** (-0.5)...  118 us
    unnamed x4, local copies, waits for them, and re-layouts  3.46 us

commit v1 on v0

--- a/solution.py
+++ b/solution.py
@@ -154,8 +154,8 @@
             copy.wait()
         for s in reversed(range(1, slots)):
             ok = direct[s]
-            if h >= ahead and s != swap and relays:
-                ok = jnp.logical_and(ok, jnp.logical_not(relaying))
+            if h >= ahead and s == swap and relays:
+                ok = jnp.logical_not(relaying)
             when(ok, lambda s=s, h=h: kv_copy(s, h).start())
     own_load.wait()
     grad_copy = partner_copy(gown, goth, 0)
@@ -201,7 +201,7 @@
             there = jnp.maximum(there, pairs[0, column])
         biases.append(jnp.where(there >= 0, 0.0, MASKED).astype(F32))
     rate = scale * LOG2E
-    lag = heads
+    lag = min(3, heads)
 
     def hand_back(r, h):
         term_copy(r, h).wait_recv()
@@ -220,8 +220,9 @@
             if s and s == swap:
                 for r in relays:
                     when(hands_on[r], lambda r=r: kv_copy(r, h, swap).start())
-                    now = jnp.logical_and(jnp.logical_and(relaying, direct[r]), h + ahead < heads)
-                    when(now, lambda r=r: kv_copy(r, h + ahead).start())
+                if relays:
+                    now = jnp.logical_and(relaying, h + ahead < heads)
+                    when(now, lambda: kv_copy(swap, h + ahead).start())
             scores = dot(kv[h, s, 0], q, 1, 1)
             probs[s] = scores
             peak = jnp.max(scores, axis=0, keepdims=True) + biases[s]

time: 122 us -> 115 us (0.943)
  the two profiles are of different devices: /device:TPU:0 before, /device:TPU:8 now
where the time goes in v1:
time: 115 us; the launch traced here: 113 us
  Pallas kernels  109 us (95%)
  local copies, waits for them, and re-layouts  3.46 us (3%)
    pallas_call x1, Pallas kernels, on_device(): pl.pallas_call(functools.partial(kernel, groups, tile_count, HD ** (-0.5)...  109 us
    unnamed x4, local copies, waits for them, and re-layouts  3.46 us

profile of v1, /device:TPU:8, one launch (start us, length us, event | category | flops | bytes accessed | tf_op | source)
XLA Modules:
  0.0 113.3 jit_solution(7615473700136279301)
XLA Ops:
  0.6 109.2 %tile_attention.1 = (bf16[384,1536]{1,0:T(8,128)(2,1)S(1)}, bf16[384,768]{1,0:T(8,128)(2,1)S(1)}, bf16[384,768]{1,0:T(8,128)(2,1)S(1)}, bf16[384,768]{1,0:T(8,128)(2,1)S(1)}) custom-call(s32[1,7]{1,0:T(1,128)} %pairs.1, bf16[384,768]{1,0:T(8,128)(2,1)} %q_in.1, bf16[384,768]{1,0:T(8,128)(2,1)} %k_in.1, bf16[384,768]{1,0:T(8,128)(2,1)} %v_in.1, ...), custom_call_target="tpu_custom_call" | custom-call | tf_op jit(solution)/shard_map/tile_attention/pallas_call | solution.py:348
  109.8 1.0 copy.14
  110.8 0.8 copy.15
  111.6 0.8 copy.16
  112.5 0.8 copy.17

commit v2 on v1

--- a/solution.py
+++ b/solution.py
@@ -39,9 +39,9 @@
 
 def kernel(
     groups, tile_count, scale,
-    pairs, q_in, k_in, v_in, w_in, g_in,
+    pairs_in, q_in, k_in, v_in, w_in, g_in,
     mixed, gq, gk, gv,
-    kv, qb, wb, gown, goth, gacc, dob, att, probs, acc, tsend, trecv, msend, mrecv,
+    pairs, kv, qb, wb, gown, goth, gacc, dob, att, probs, acc, tsend, trecv, msend, mrecv,
     load_sem, kv_send, kv_recv, t_send, t_recv, x_send, x_recv,
 ):
     g = lax.axis_index("seq")
@@ -124,6 +124,7 @@
             (load(k_in.at[:, cols], kv.at[h, 0, 0]), load(v_in.at[:, cols], kv.at[h, 0, 1]))
         )
     own_load = load(g_in, gown)
+    pairs_load = load(pairs_in, pairs)
     w_load = load(w_in, wb)
     q_loads = [load(q_in.at[:, pl.ds(h * HD, HD)], qb.at[h]) for h in range(heads)]
 
@@ -194,6 +195,7 @@
     for copy in q_loads:
         copy.wait()
 
+    pairs_load.wait()
     biases = []
     for _, _, columns in groups:
         there = pairs[0, columns[0]]
@@ -202,6 +204,9 @@
         biases.append(jnp.where(there >= 0, 0.0, MASKED).astype(F32))
     rate = scale * LOG2E
     lag = min(3, heads)
+    hold = min(2, heads)
+    late = 2 * lax.rem(g, middle) >= middle
+    holding = jnp.logical_and(late, jnp.logical_not(relaying)) if relays else late
 
     def hand_back(r, h):
         term_copy(r, h).wait_recv()
@@ -262,15 +267,30 @@
         gq[:, cols] = (gq_t * scale).T.astype(BF16)
         for s in reversed(range(1, slots)):
             ok = source[s][1]
-            if s == swap and relays:
-                ok = jnp.logical_not(relaying)
+            if s == swap:
+                ok = jnp.logical_not(late)
+                if relays:
+                    ok = jnp.logical_and(ok, jnp.logical_not(relaying))
             when(ok, lambda s=s: term_copy(s, h).start())
+        if swap is not None:
+            now = jnp.logical_and(holding, h >= hold)
+            when(now, lambda: term_copy(swap, h - hold).start())
         for r in relays:
             now = jnp.logical_and(hands_on[r], h >= lag)
             when(now, lambda r=r: hand_back(r, h - lag))
         return carry
 
     lax.fori_loop(0, heads, head, 0)
+
+    def send_rest():
+        def body(h, carry):
+            term_copy(swap, h).start()
+            return carry
+
+        lax.fori_loop(heads - hold, heads, body, 0)
+
+    if swap is not None:
+        when(holding, send_rest)
 
     def hand_back_rest(r):
         def body(h, carry):
@@ -332,6 +352,18 @@
         return carry
 
     lax.fori_loop(0, heads, drain, 0)
+
+
+def write_out(*refs):
+    sems = refs[-1]
+    copies = [
+        pltpu.make_async_copy(src, dst, sems.at[i])
+        for i, (src, dst) in enumerate(zip(refs[:4], refs[4:8]))
+    ]
+    for copy in copies:
+        copy.start()
+    for copy in copies:
+        copy.wait()
 
 
 def on_device(query_tok, key_tok, value_tok, out_weight, grad_out, tile_pairs):
@@ -345,7 +377,7 @@
     in_vmem = pl.BlockSpec(memory_space=pltpu.VMEM)
     dma = pltpu.SemaphoreType.DMA
     near = (slots - 1, heads)
-    return pl.pallas_call(
+    held = pl.pallas_call(
         functools.partial(kernel, groups, tile_count, HD ** (-0.5)),
         out_shape=(
             pltpu.VMEM((rows, half), BF16),
@@ -353,9 +385,10 @@
             pltpu.VMEM((rows, width), BF16),
             pltpu.VMEM((rows, width), BF16),
         ),
-        in_specs=[pl.BlockSpec(memory_space=pltpu.SMEM)] + [anywhere] * 5,
+        in_specs=[anywhere] * 6,
         out_specs=(in_vmem,) * 4,
         scratch_shapes=[
+            pltpu.SMEM(tile_pairs.shape, jnp.int32),
             pltpu.VMEM((heads, slots, 2, rows, HD), BF16),
             pltpu.VMEM((heads, rows, HD), BF16),
             pltpu.VMEM(out_weight.shape, BF16),
@@ -370,7 +403,7 @@
             pltpu.VMEM(near + (2, rows, HD), BF16),
             pltpu.VMEM((rows, half), BF16),
             pltpu.VMEM((rows, half), BF16),
-            dma((3 * heads + 2,)),
+            dma((3 * heads + 3,)),
             dma(near),
             dma(near),
             dma(near),
@@ -383,6 +416,14 @@
         ),
         name="tile_attention",
     )(tile_pairs, query_tok, key_tok, value_tok, out_weight, grad_out)
+    return pl.pallas_call(
+        write_out,
+        out_shape=tuple(jax.ShapeDtypeStruct(x.shape, x.dtype) for x in held),
+        in_specs=[in_vmem] * 4,
+        out_specs=(anywhere,) * 4,
+        scratch_shapes=[dma((4,))],
+        name="write_out",
+    )(*[pltpu.with_memory_space_constraint(x, pltpu.VMEM) for x in held])
 
 
 def solution(mesh):

time: 115 us -> 111 us (0.965); the launches traced: 113 us -> 111 us
  local copies, waits for them, and re-layouts: 3.46 us -> 0 us
    unnamed x4 -> x0, local copies, waits for them, and re-layouts: 3.46 us -> none
    pallas_call x0 -> x1, Pallas kernels: none -> 1.63 us  [on_device(): pl.pallas_call(write_out, out_shape=tuple((jax.ShapeDtypeStruct(x.shape,...]
where the time goes in v2:
time: 111 us
  Pallas kernels  110 us (99%)
    pallas_call x1, Pallas kernels, on_device(): pl.pallas_call(functools.partial(kernel, groups, tile_count, HD ** (-0.5)...  109 us

profile of v2, /device:TPU:8, one launch (start us, length us, event | category | flops | bytes accessed | tf_op | source)
XLA Modules:
  0.0 110.8 jit_solution(12144366367408384064)
XLA Ops:
  0.6 108.6 %tile_attention.1 = (bf16[384,1536]{1,0:T(8,128)(2,1)S(1)}, bf16[384,768]{1,0:T(8,128)(2,1)S(1)}, bf16[384,768]{1,0:T(8,128)(2,1)S(1)}, bf16[384,768]{1,0:T(8,128)(2,1)S(1)}) custom-call(s32[1,7]{1,0:T(1,128)} %pairs_in.1, bf16[384,768]{1,0:T(8,128)(2,1)} %q_in.1, bf16[384,768]{1,0:T(8,128)(2,1)} %k_in.1, bf16[384,768]{1,0:T(8,128)(2,1)} %v_in.1, ...), custom_call_target="tpu_custom_call" | custom-call | tf_op jit(solution)/shard_map/tile_attention/pallas_call | solution.py:380
  109.2 1.6 %write_out.1 = (bf16[384,1536]{1,0:T(8,128)(2,1)}, bf16[384,768]{1,0:T(8,128)(2,1)}, bf16[384,768]{1,0:T(8,128)(2,1)}, bf16[384,768]{1,0:T(8,128)(2,1)}) custom-call(bf16[384,1536]{1,0:T(8,128)(2,1)S(1)} %get-tuple-element.8.refs_0_, bf16[384,768]{1,0:T(8,128)(2,1)S(1)} %get-tuple-element.9.refs_1_, bf16[384,768]{1,0:T(8,128)(2,1)S(1)} %get-tuple-element.10.refs_2_, ...), custom_call_target="tpu_custom_call" | custom-call | tf_op jit(solution)/shard_map/write_out/pallas_call | solution.py:419

commit v3 on v2

--- a/solution.py
+++ b/solution.py
@@ -42,7 +42,7 @@
     pairs_in, q_in, k_in, v_in, w_in, g_in,
     mixed, gq, gk, gv,
     pairs, kv, qb, wb, gown, goth, gacc, dob, att, probs, acc, tsend, trecv, msend, mrecv,
-    load_sem, kv_send, kv_recv, t_send, t_recv, x_send, x_recv,
+    ready, load_sem, kv_send, kv_recv, t_send, t_recv, x_send, x_recv,
 ):
     g = lax.axis_index("seq")
     c = lax.axis_index("head")
@@ -101,13 +101,22 @@
     barrier = pltpu.get_barrier_semaphore()
     pl.semaphore_signal(barrier, inc=1, device_id=(g, other), device_id_type=MESH)
     peers = 1
-    for to, ok in target[1:] + source[1:]:
+    answers = [(0, middle - 1), (middle, tile_count - 1)]
+    if middle >= 4:
+        answers.append((middle + middle // 2, middle + middle // 2 - 1))
+    if not relays:
+        answers = []
+    for to, ok in target[1:] + [source[s] for s in range(1, slots) if s != swap]:
+        greets, counts = ok, ok
+        for early, late in answers:
+            greets = jnp.logical_and(greets, jnp.logical_not((g == late) & (to == early))) if ok is not None else None
+            counts = jnp.logical_and(counts, jnp.logical_not((g == early) & (to == late))) if ok is not None else None
 
         def greet(to=to):
             pl.semaphore_signal(barrier, inc=1, device_id=(to, c), device_id_type=MESH)
 
-        when(ok, greet)
-        peers = peers + (1 if ok is None else ok.astype(jnp.int32))
+        when(greets, greet)
+        peers = peers + (1 if counts is None else counts.astype(jnp.int32))
 
     loads = []
 
@@ -129,6 +138,15 @@
     q_loads = [load(q_in.at[:, pl.ds(h * HD, HD)], qb.at[h]) for h in range(heads)]
 
     pl.semaphore_wait(barrier, peers)
+    for early, late in answers:
+
+        def answer(early=early):
+            pl.semaphore_signal(ready, inc=1, device_id=(early, c), device_id_type=MESH)
+
+        pl.when(g == late)(answer)
+
+    def hear():
+        pl.semaphore_wait(ready, 1)
 
     def partner_copy(src, dst, i):
         return pltpu.make_async_remote_copy(
@@ -150,14 +168,29 @@
             device_id=(source[s][0], c), device_id_type=MESH,
         )
 
+    def send_swap_tile(h, side=None):
+        if swap is None or h >= heads:
+            return
+        ok = side
+        if h >= ahead and relays:
+            ok = jnp.logical_not(relaying)
+            ok = ok if side is None else jnp.logical_and(side, ok)
+        when(ok, lambda: kv_copy(swap, h).start())
+
+    for copy in kv_loads[0]:
+        copy.wait()
+    send_swap_tile(0)
+    if len(answers) > 2:
+        pl.when(g == answers[2][0])(hear)
     for h in range(heads):
-        for copy in kv_loads[h]:
-            copy.wait()
+        if h + 1 < heads:
+            for copy in kv_loads[h + 1]:
+                copy.wait()
+        send_swap_tile(h + 1, c == 0)
         for s in reversed(range(1, slots)):
-            ok = direct[s]
-            if h >= ahead and s == swap and relays:
-                ok = jnp.logical_not(relaying)
-            when(ok, lambda s=s, h=h: kv_copy(s, h).start())
+            if s != swap:
+                when(direct[s], lambda s=s, h=h: kv_copy(s, h).start())
+        send_swap_tile(h + 1, c != 0)
     own_load.wait()
     grad_copy = partner_copy(gown, goth, 0)
     grad_copy.start()
@@ -192,6 +225,8 @@
         return carry
 
     lax.fori_loop(0, heads, grad_other, 0)
+    if answers:
+        pl.when(jnp.logical_or(g == answers[0][0], g == answers[1][0]))(hear)
     for copy in q_loads:
         copy.wait()
 
@@ -204,7 +239,7 @@
         biases.append(jnp.where(there >= 0, 0.0, MASKED).astype(F32))
     rate = scale * LOG2E
     lag = min(3, heads)
-    hold = min(2, heads)
+    hold = min(1, heads)
     late = 2 * lax.rem(g, middle) >= middle
     holding = jnp.logical_and(late, jnp.logical_not(relaying)) if relays else late
 
@@ -265,16 +300,21 @@
             part = dot(kv[h, s, 0], gs, 0, 0)
             gq_t = part if gq_t is None else gq_t + part
         gq[:, cols] = (gq_t * scale).T.astype(BF16)
+        def send_swap_term(side):
+            if swap is None:
+                return
+            ok = jnp.logical_and(side, jnp.logical_not(late))
+            if relays:
+                ok = jnp.logical_and(ok, jnp.logical_not(relaying))
+            pl.when(ok)(lambda: term_copy(swap, h).start())
+            now = jnp.logical_and(jnp.logical_and(side, holding), h >= hold)
+            pl.when(now)(lambda: term_copy(swap, h - hold).start())
+
+        send_swap_term(c != 0)
         for s in reversed(range(1, slots)):
-            ok = source[s][1]
-            if s == swap:
-                ok = jnp.logical_not(late)
-                if relays:
-                    ok = jnp.logical_and(ok, jnp.logical_not(relaying))
-            when(ok, lambda s=s: term_copy(s, h).start())
-        if swap is not None:
-            now = jnp.logical_and(holding, h >= hold)
-            when(now, lambda: term_copy(swap, h - hold).start())
+            if s != swap:
+                when(source[s][1], lambda s=s: term_copy(s, h).start())
+        send_swap_term(c == 0)
         for r in relays:
             now = jnp.logical_and(hands_on[r], h >= lag)
             when(now, lambda r=r: hand_back(r, h - lag))
@@ -403,6 +443,7 @@
             pltpu.VMEM(near + (2, rows, HD), BF16),
             pltpu.VMEM((rows, half), BF16),
             pltpu.VMEM((rows, half), BF16),
+            pltpu.SemaphoreType.REGULAR,
             dma((3 * heads + 3,)),
             dma(near),
             dma(near),
@@ -415,7 +456,7 @@
             collective_id=0, has_side_effects=True, vmem_limit_bytes=52 * 2**20
         ),
         name="tile_attention",
-    )(tile_pairs, query_tok, key_tok, value_tok, out_weight, grad_out)
+    )(pltpu.with_memory_space_constraint(tile_pairs, pltpu.HBM), query_tok, key_tok, value_tok, out_weight, grad_out)
     return pl.pallas_call(
         write_out,
         out_shape=tuple(jax.ShapeDtypeStruct(x.shape, x.dtype) for x in held),

time: 111 us -> 110 us (level)
  no operation moved by 1% of the time
where the time goes in v3:
time: 110 us
  Pallas kernels  109 us (99%)
    pallas_call x1, Pallas kernels, on_device(): pl.pallas_call(functools.partial(kernel, groups, tile_count, HD ** (-0.5)...  108 us

profile of v3, /device:TPU:8, one launch (start us, length us, event | category | flops | bytes accessed | tf_op | source)
XLA Modules:
  0.0 110.0 jit_solution(17536281091303788867)
XLA Ops:
  0.6 107.7 %tile_attention.1 = (bf16[384,1536]{1,0:T(8,128)(2,1)S(1)}, bf16[384,768]{1,0:T(8,128)(2,1)S(1)}, bf16[384,768]{1,0:T(8,128)(2,1)S(1)}, bf16[384,768]{1,0:T(8,128)(2,1)S(1)}) custom-call(s32[1,7]{1,0:T(1,128)} %pairs_in.1, bf16[384,768]{1,0:T(8,128)(2,1)} %q_in.1, bf16[384,768]{1,0:T(8,128)(2,1)} %k_in.1, bf16[384,768]{1,0:T(8,128)(2,1)} %v_in.1, ...), custom_call_target="tpu_custom_call" | custom-call | tf_op jit(solution)/shard_map/tile_attention/pallas_call | solution.py:420
  108.3 1.6 %write_out.1 = (bf16[384,1536]{1,0:T(8,128)(2,1)}, bf16[384,768]{1,0:T(8,128)(2,1)}, bf16[384,768]{1,0:T(8,128)(2,1)}, bf16[384,768]{1,0:T(8,128)(2,1)}) custom-call(bf16[384,1536]{1,0:T(8,128)(2,1)S(1)} %get-tuple-element.8.refs_0_, bf16[384,768]{1,0:T(8,128)(2,1)S(1)} %get-tuple-element.9.refs_1_, bf16[384,768]{1,0:T(8,128)(2,1)S(1)} %get-tuple-element.10.refs_2_, ...), custom_call_target="tpu_custom_call" | custom-call | tf_op jit(solution)/shard_map/write_out/pallas_call | solution.py:460

commit v4 on v3

--- a/solution.py
+++ b/solution.py
@@ -241,6 +241,7 @@
     lag = min(3, heads)
     hold = min(1, heads)
     late = 2 * lax.rem(g, middle) >= middle
+    late = jnp.logical_and(late, jnp.logical_or(g != middle + middle // 2, c == 0))
     holding = jnp.logical_and(late, jnp.logical_not(relaying)) if relays else late
 
     def hand_back(r, h):

time: 110 us -> 110 us (level)
  no operation moved by 1% of the time
where the time goes in v4:
time: 110 us
  Pallas kernels  109 us (99%)
    pallas_call x1, Pallas kernels, on_device(): pl.pallas_call(functools.partial(kernel, groups, tile_count, HD ** (-0.5)...  108 us

profile of v4, /device:TPU:8, one launch (start us, length us, event | category | flops | bytes accessed | tf_op | source)
XLA Modules:
  0.0 110.0 jit_solution(8651387275598591751)
XLA Ops:
  0.6 107.7 %tile_attention.1 = (bf16[384,1536]{1,0:T(8,128)(2,1)S(1)}, bf16[384,768]{1,0:T(8,128)(2,1)S(1)}, bf16[384,768]{1,0:T(8,128)(2,1)S(1)}, bf16[384,768]{1,0:T(8,128)(2,1)S(1)}) custom-call(s32[1,7]{1,0:T(1,128)} %pairs_in.1, bf16[384,768]{1,0:T(8,128)(2,1)} %q_in.1, bf16[384,768]{1,0:T(8,128)(2,1)} %k_in.1, bf16[384,768]{1,0:T(8,128)(2,1)} %v_in.1, ...), custom_call_target="tpu_custom_call" | custom-call | tf_op jit(solution)/shard_map/tile_attention/pallas_call | solution.py:421
  108.4 1.6 %write_out.1 = (bf16[384,1536]{1,0:T(8,128)(2,1)}, bf16[384,768]{1,0:T(8,128)(2,1)}, bf16[384,768]{1,0:T(8,128)(2,1)}, bf16[384,768]{1,0:T(8,128)(2,1)}) custom-call(bf16[384,1536]{1,0:T(8,128)(2,1)S(1)} %get-tuple-element.8.refs_0_, bf16[384,768]{1,0:T(8,128)(2,1)S(1)} %get-tuple-element.9.refs_1_, bf16[384,768]{1,0:T(8,128)(2,1)S(1)} %get-tuple-element.10.refs_2_, ...), custom_call_target="tpu_custom_call" | custom-call | tf_op jit(solution)/shard_map/write_out/pallas_call | solution.py:461
